TPU v7x, 32 devices: a whole 2x2x4 slice. The times are simulated.
32 devices in a mesh: shard: 4 (over z), context: 2 (over x), tensor: 4 (over y, core).
Axes of the slice: x: 2, y: 2, z: 4, core: 2. Of those that a mesh axis runs over, the one named last changes fastest.
Arguments:
- hidden_in: bfloat16 [4, 2048, 1536], P('shard', 'context'), may hold values from -6 to 6
- norm_gain: float32 [1536], replicated, may hold values from 0.5 to 1.5
- w_in_zx: bfloat16 [1536, 2, 3072], P('shard', None, 'tensor'), may hold values from -0.15625 to 0.15625
- w_in_bc: bfloat16 [1536, 256], P('shard'), may hold values from -0.15625 to 0.15625
- w_in_dt: bfloat16 [1536, 48], P('shard', 'tensor'), may hold values from -0.15625 to 0.15625
- conv_x: float32 [5, 3072], P(None, 'tensor'), may hold values from -3 to 3
- conv_bc: float32 [5, 256], replicated, may hold values from -3 to 3
- dt_bias: float32 [48], P('tensor'), may hold values from -6 to -2.5
- a_log: float32 [48], P('tensor'), may hold values from -1 to 1.5
- d_skip: float32 [48], P('tensor'), may hold values from 0.5 to 1.5
- out_gain: float32 [3072], P('tensor'), may hold values from 0.5 to 1.5
- w_out: bfloat16 [3072, 1536], P('tensor', 'shard'), may hold values from -0.109375 to 0.109375
- cotangent: bfloat16 [4, 2048, 1536], P('shard', 'context'), may hold values from -6 to 6
Outputs:
- out: bfloat16 [4, 2048, 1536], P('shard', 'context')
- grad_in: float32 [4, 2048, 1536], P('shard', 'context')
- grad_norm_gain: float32 [1536], replicated
- grad_w_in_zx: float32 [1536, 2, 3072], P(('shard', 'context'), None, 'tensor')
- grad_w_in_bc: float32 [1536, 256], P(('shard', 'context'))
- grad_w_in_dt: float32 [1536, 48], P(('shard', 'context'), 'tensor')
- grad_conv_x: float32 [5, 3072], P(None, 'tensor')
- grad_conv_bc: float32 [5, 256], replicated
- grad_dt_bias: float32 [48], P('tensor')
- grad_a_log: float32 [48], P('tensor')
- grad_d_skip: float32 [48], P('tensor')
- grad_out_gain: float32 [3072], P('tensor')
- grad_w_out: float32 [3072, 1536], P('tensor', ('shard', 'context'))
- rms_stream: float32 [], replicated
- rms_mixer: float32 [], replicated
All inputs are finite; a program needn't handle non-finite values.
Results may differ from a plain program's by a relative error of at most 0.012.
Values may be sent and summed in bfloat16 or wider, within the bound.
No kernel may reach another device: no remote copies, remote signals or barrier semaphores. Data moves between devices by JAX's collectives and lax.ppermute only.
A program may use at most 192 MiB of HBM per device.

v0:
```python
import jax
import jax.numpy as jnp
from jax import lax
from jax.sharding import PartitionSpec as P

CH = 256
EPSILON = 1e-05
PRECISE = lax.Precision.HIGHEST


def shifted(array, axis, by):
    length = lax.axis_size(axis)
    pairs = [(i, i + by) for i in range(length) if 0 <= i + by < length]
    return lax.ppermute(array, axis, pairs)


def carried_in(array, axis, combine, identity, reverse):
    length, place = (lax.axis_size(axis), lax.axis_index(axis))
    everything = jax.tree.map(lambda part: lax.all_gather(part, axis), array)
    start = jax.tree.map(
        lambda part, zero: jnp.broadcast_to(jnp.asarray(zero, part.dtype), part.shape),
        array,
        identity,
    )

    def hop(k, before):
        at = length - 1 - k if reverse else k
        reached = at > place if reverse else at < place
        new = combine(before, jax.tree.map(lambda part: part[at], everything))
        return jax.tree.map(lambda a, b: jnp.where(reached, a, b), new, before)

    return lax.fori_loop(0, length, hop, start)


def combine_states(earlier, nearer):
    return (earlier[0] * nearer[0], nearer[0][..., None, None] * earlier[1] + nearer[1])


def silu_grad(values, sigmoid_val):
    return sigmoid_val * (1.0 + values * (1.0 - sigmoid_val))


def contract_rows(left_op, right_op):
    return lax.dot_general(
        left_op, right_op, (((0,), (0,)), ((), ())), preferred_element_type=jnp.float32
    )


def contract_cols(left_op, right_op):
    return lax.dot_general(
        left_op, right_op, (((1,), (1,)), ((), ())), preferred_element_type=jnp.float32
    )


def reverse_cumsum(values, axis_num):
    return jnp.flip(jnp.cumsum(jnp.flip(values, axis_num), axis=axis_num), axis_num)


def advance(running, element):
    return (element[0][..., None, None] * running + element[1], running)


def retreat(running, element):
    return (element[1] + element[0][..., None, None] * running, running)


def on_device(
    hidden_in,
    norm_gain,
    w_in_zx,
    w_in_bc,
    w_in_dt,
    conv_x,
    conv_bc,
    dt_bias,
    a_log,
    d_skip,
    out_gain,
    w_out,
    cotangent,
):
    seq_count, local_len, model_dim = hidden_in.shape
    inner_dev = w_in_zx.shape[2]
    heads_dev = w_in_dt.shape[1]
    head_dim = inner_dev // heads_dev
    state_dim = w_in_bc.shape[1] // 2
    tap_count = conv_x.shape[0] - 1
    inner_all = inner_dev * lax.axis_size("tensor")
    block_len = CH
    block_count = local_len // block_len
    row_count = seq_count * local_len
    channels = inner_dev + 2 * state_dim
    zx_full, bc_full, dt_full, out_full = (
        lax.all_gather(w_in_zx, "shard", axis=0, tiled=True),
        lax.all_gather(w_in_bc, "shard", axis=0, tiled=True),
        lax.all_gather(w_in_dt, "shard", axis=0, tiled=True),
        lax.all_gather(w_out, "shard", axis=1, tiled=True),
    )
    zx_mat = zx_full.reshape(model_dim, 2 * inner_dev)
    stream_in = hidden_in.reshape(row_count, model_dim).astype(jnp.float32)
    scale_in = lax.rsqrt(jnp.mean(stream_in * stream_in, axis=-1, keepdims=True) + EPSILON)
    normed = (stream_in * scale_in * norm_gain).astype(jnp.bfloat16)
    zx_val = jnp.dot(normed, zx_mat, preferred_element_type=jnp.float32)
    gate_val = zx_val[:, :inner_dev]
    bc_val = jnp.dot(normed, bc_full, preferred_element_type=jnp.float32)
    dt_raw = jnp.dot(normed, dt_full, preferred_element_type=jnp.float32)
    pre_conv = jnp.concatenate([zx_val[:, inner_dev:], bc_val], axis=-1).reshape(
        seq_count, local_len, channels
    )
    prev_rows = shifted(pre_conv[:, local_len - tap_count + 1 :], "context", 1)
    padded = jnp.concatenate([prev_rows, pre_conv], axis=1)
    conv_all = jnp.concatenate([conv_x, conv_bc], axis=1)
    conv_out = conv_all[tap_count] + conv_all[0] * padded[:, 0:local_len]
    for tap_idx in range(1, tap_count):
        conv_out = conv_out + conv_all[tap_idx] * padded[:, tap_idx : tap_idx + local_len]
    sig_conv = jax.nn.sigmoid(conv_out)
    activated = (conv_out * sig_conv).astype(jnp.bfloat16)
    xa_blk = activated[..., :inner_dev].reshape(
        seq_count, block_count, block_len, heads_dev, head_dim
    )
    bm_blk = activated[..., inner_dev : inner_dev + state_dim].reshape(
        seq_count, block_count, block_len, state_dim
    )
    cm_blk = activated[..., inner_dev + state_dim :].reshape(
        seq_count, block_count, block_len, state_dim
    )
    xa_f = xa_blk.astype(jnp.float32)
    bm_f = bm_blk.astype(jnp.float32)
    cm_f = cm_blk.astype(jnp.float32)
    dt_pre = dt_raw + dt_bias
    dt_val = jax.nn.softplus(dt_pre)
    rate_neg = -jnp.exp(a_log)
    dt_q = dt_val.reshape(seq_count, block_count, block_len, heads_dev)
    log_q = (dt_val * rate_neg).reshape(seq_count, block_count, block_len, heads_dev)
    cum_q = jnp.cumsum(log_q, axis=2)
    block_log = cum_q[:, :, -1]
    cum_t = jnp.swapaxes(cum_q, 2, 3)
    dt_t = jnp.swapaxes(dt_q, 2, 3)
    positions = jnp.arange(block_len)
    lower_mask = positions[:, None] >= positions[None, :]
    log_gap = cum_t[..., :, None] - cum_t[..., None, :]
    decay_mat = jnp.exp(jnp.where(lower_mask, log_gap, 0.0)) * lower_mask.astype(jnp.float32)
    scores = jnp.einsum("scin,scjn->scij", cm_blk, bm_blk, preferred_element_type=jnp.float32)
    weights_f = scores[:, :, None] * decay_mat * dt_t[..., None, :]
    weights_b = weights_f.astype(jnp.bfloat16)
    y_intra = jnp.einsum(
        "schij,scjhp->scihp", weights_b, xa_blk, preferred_element_type=jnp.float32
    )
    w_end = jnp.exp(block_log[:, :, None, :] - cum_q) * dt_q
    xw_val = (xa_f * w_end[..., None]).astype(jnp.bfloat16)
    state_add = jnp.einsum("scjn,scjhp->schnp", bm_blk, xw_val, preferred_element_type=jnp.float32)
    block_decay = jnp.exp(block_log)
    zero_state = jnp.zeros((seq_count, heads_dev, state_dim, head_dim), jnp.float32)
    end_local, start_local = lax.scan(
        advance, zero_state, (jnp.moveaxis(block_decay, 1, 0), jnp.moveaxis(state_add, 1, 0))
    )
    start_local = jnp.moveaxis(start_local, 0, 1)
    dev_decay = jnp.prod(block_decay, axis=1)
    _, in_state = carried_in(
        (dev_decay, end_local),
        "context",
        combine_states,
        (jnp.ones_like(dev_decay), jnp.zeros_like(end_local)),
        False,
    )
    before_dec = jnp.exp(jnp.cumsum(block_log, axis=1) - block_log)
    start_state = start_local + before_dec[..., None, None] * in_state[:, None]
    start_b = start_state.astype(jnp.bfloat16)
    cum_exp = jnp.exp(cum_q)
    cm_scaled = (cm_f[:, :, :, None, :] * cum_exp[..., None]).astype(jnp.bfloat16)
    y_inter = jnp.einsum(
        "scihn,schnp->scihp", cm_scaled, start_b, preferred_element_type=jnp.float32
    )
    y_ssd = (y_intra + y_inter + d_skip[:, None] * xa_f).reshape(row_count, inner_dev)
    sig_gate = jax.nn.sigmoid(gate_val)
    silu_gate = gate_val * sig_gate
    gated = y_ssd * silu_gate
    square_sum = lax.psum(jnp.sum(gated * gated, axis=-1), "tensor")
    scale_out = lax.rsqrt(square_sum / inner_all + EPSILON)[:, None]
    out_in = (gated * scale_out * out_gain).astype(jnp.bfloat16)
    mixed = lax.psum(jnp.dot(out_in, out_full, preferred_element_type=jnp.float32), "tensor")
    stream = stream_in + mixed
    stream_sq = jnp.sum(stream * stream)
    mixed_sq = jnp.sum(mixed * mixed)
    grad_rows = cotangent.reshape(row_count, model_dim)
    grad_stream = grad_rows.astype(jnp.float32)
    grad_wout = contract_rows(out_in, grad_rows)
    wout_share = lax.psum_scatter(grad_wout, ("shard", "context"), scatter_dimension=1, tiled=True)
    grad_on = contract_cols(grad_rows, out_full)
    grad_og = jnp.sum(grad_on * gated * scale_out, axis=0)
    grad_gn = grad_on * out_gain
    dot_sum = lax.psum(jnp.sum(grad_gn * gated, axis=-1), "tensor")
    grad_gated = scale_out * grad_gn - gated * scale_out**3 * (dot_sum / inner_all)[:, None]
    grad_y = (grad_gated * silu_gate).astype(jnp.bfloat16)
    grad_gate = (grad_gated * y_ssd * silu_grad(gate_val, sig_gate)).astype(jnp.bfloat16)
    grad_yb = grad_y.reshape(seq_count, block_count, block_len, heads_dev, head_dim)
    grad_yf = grad_yb.astype(jnp.float32)
    grad_wts = jnp.einsum("scihp,scjhp->schij", grad_yb, xa_blk, preferred_element_type=jnp.float32)
    grad_xa = (
        jnp.einsum("schij,scihp->scjhp", weights_b, grad_yb, preferred_element_type=jnp.float32)
        + d_skip[:, None] * grad_yf
    )
    grad_skip = jnp.sum(grad_yf * xa_f, axis=(0, 1, 2, 4))
    weighted = grad_wts * weights_f
    grad_cum_t = jnp.sum(weighted, axis=-1) - jnp.sum(weighted, axis=-2)
    grad_dt_t = jnp.sum(grad_wts * scores[:, :, None] * decay_mat, axis=-2)
    grad_scores = jnp.sum(grad_wts * decay_mat * dt_t[..., None, :], axis=2)
    grad_bm = jnp.einsum("scij,scin->scjn", grad_scores, cm_f, precision=PRECISE)
    grad_cm = jnp.einsum("scij,scjn->scin", grad_scores, bm_f, precision=PRECISE)
    grad_scaled = jnp.einsum(
        "scihp,schnp->scihn", grad_yb, start_b, preferred_element_type=jnp.float32
    )
    grad_cm = grad_cm + jnp.sum(grad_scaled * cum_exp[..., None], axis=3)
    grad_cum_q = (
        jnp.swapaxes(grad_cum_t, 2, 3)
        + jnp.sum(grad_scaled * cm_f[:, :, :, None, :], axis=-1) * cum_exp
    )
    grad_start = jnp.einsum(
        "scihn,scihp->schnp", cm_scaled, grad_yb, preferred_element_type=jnp.float32
    )
    gin_local, after_local = lax.scan(
        retreat,
        zero_state,
        (jnp.moveaxis(block_decay, 1, 0), jnp.moveaxis(grad_start, 1, 0)),
        reverse=True,
    )
    after_local = jnp.moveaxis(after_local, 0, 1)
    _, grad_end = carried_in(
        (dev_decay, gin_local),
        "context",
        combine_states,
        (jnp.ones_like(dev_decay), jnp.zeros_like(gin_local)),
        True,
    )
    after_dec = jnp.exp(jnp.sum(block_log, axis=1, keepdims=True) - jnp.cumsum(block_log, axis=1))
    grad_after = after_local + after_dec[..., None, None] * grad_end[:, None]
    grad_lam = block_decay * jnp.sum(grad_after * start_state, axis=(-2, -1))
    grad_after_b = grad_after.astype(jnp.bfloat16)
    grad_xw = jnp.einsum(
        "scjn,schnp->scjhp", bm_blk, grad_after_b, preferred_element_type=jnp.float32
    )
    grad_bm = grad_bm + jnp.einsum(
        "scjhp,schnp->scjn", xw_val, grad_after_b, preferred_element_type=jnp.float32
    )
    grad_xa = grad_xa + grad_xw * w_end[..., None]
    grad_wend = jnp.sum(grad_xw * xa_f, axis=-1)
    grad_cum_q = grad_cum_q - grad_wend * w_end
    grad_lam = grad_lam + jnp.sum(grad_wend * w_end, axis=2)
    grad_dt_q = jnp.swapaxes(grad_dt_t, 2, 3) + grad_wend * jnp.exp(
        block_log[:, :, None, :] - cum_q
    )
    grad_log = reverse_cumsum(grad_cum_q, 2) + grad_lam[:, :, None, :]
    grad_dt_q = grad_dt_q + grad_log * rate_neg
    grad_alog = jnp.sum(grad_log * log_q, axis=(0, 1, 2))
    grad_raw = grad_dt_q.reshape(row_count, heads_dev) * jax.nn.sigmoid(dt_pre)
    grad_dtb = jnp.sum(grad_raw, axis=0)
    bc_part = jnp.concatenate([grad_bm, grad_cm], axis=-1).reshape(row_count, 2 * state_dim)
    bc_sum = lax.psum(bc_part, "tensor")
    grad_act = jnp.concatenate(
        [
            grad_xa.reshape(seq_count, local_len, inner_dev),
            bc_sum.reshape(seq_count, local_len, 2 * state_dim),
        ],
        axis=-1,
    )
    grad_conv = grad_act * silu_grad(conv_out, sig_conv)
    next_rows = shifted(grad_conv[:, : tap_count - 1], "context", -1)
    extended = jnp.concatenate([grad_conv, next_rows], axis=1)
    grad_pre = conv_all[0] * extended[:, tap_count - 1 : tap_count - 1 + local_len]
    for tap_idx in range(1, tap_count):
        start_at = tap_count - 1 - tap_idx
        grad_pre = grad_pre + conv_all[tap_idx] * extended[:, start_at : start_at + local_len]
    taps_grad = [
        jnp.sum(grad_conv * padded[:, tap_idx : tap_idx + local_len], axis=(0, 1))
        for tap_idx in range(tap_count)
    ]
    grad_taps = jnp.stack(taps_grad + [jnp.sum(grad_conv, axis=(0, 1))], axis=0)
    grad_pre_rows = grad_pre.reshape(row_count, channels)
    grad_zx = jnp.concatenate(
        [grad_gate, grad_pre_rows[:, :inner_dev].astype(jnp.bfloat16)], axis=-1
    )
    grad_bc = grad_pre_rows[:, inner_dev:].astype(jnp.bfloat16)
    grad_raw_b = grad_raw.astype(jnp.bfloat16)
    grad_wzx = contract_rows(normed, grad_zx).reshape(model_dim, 2, inner_dev)
    grad_wbc = contract_rows(normed, grad_bc)
    grad_wdt = contract_rows(normed, grad_raw_b)
    part_in = contract_cols(grad_zx, zx_mat) + contract_cols(grad_raw_b, dt_full)
    grad_normed = lax.psum(part_in, "tensor") + contract_cols(grad_bc, bc_full)
    grad_ng = jnp.sum(grad_normed * stream_in * scale_in, axis=0)
    grad_un = grad_normed * norm_gain
    grad_input = (
        grad_stream
        + scale_in * grad_un
        - stream_in * scale_in**3 * jnp.mean(grad_un * stream_in, axis=-1, keepdims=True)
    )
    summed = lax.psum(
        (
            grad_ng,
            grad_taps[:, :inner_dev],
            grad_taps[:, inner_dev:],
            grad_dtb,
            grad_alog,
            grad_skip,
            grad_og,
            jnp.stack([stream_sq, mixed_sq]),
        ),
        ("shard", "context"),
    )
    zx_share, bc_share, dt_share = (
        lax.psum_scatter(grad_wzx, ("shard", "context"), scatter_dimension=0, tiled=True),
        lax.psum_scatter(grad_wbc, ("shard", "context"), scatter_dimension=0, tiled=True),
        lax.psum_scatter(grad_wdt, ("shard", "context"), scatter_dimension=0, tiled=True),
    )
    entry_count = row_count * model_dim * lax.axis_size("shard") * lax.axis_size("context")
    square_totals = summed[7]
    return (
        stream.astype(jnp.bfloat16).reshape(hidden_in.shape),
        grad_input.reshape(hidden_in.shape),
        summed[0],
        zx_share,
        bc_share,
        dt_share,
        summed[1],
        summed[2],
        summed[3],
        summed[4],
        summed[5],
        summed[6],
        wout_share,
        jnp.sqrt(square_totals[0] / entry_count),
        jnp.sqrt(square_totals[1] / entry_count),
    )


def solution(mesh):
    placed = (
        P("shard", "context", None),
        P(),
        P("shard", None, "tensor"),
        P("shard", None),
        P("shard", "tensor"),
        P(None, "tensor"),
        P(),
        P("tensor"),
        P("tensor"),
        P("tensor"),
        P("tensor"),
        P("tensor", "shard"),
        P("shard", "context", None),
    )
    return jax.shard_map(
        on_device,
        mesh=mesh,
        in_specs=placed,
        out_specs=(
            P("shard", "context", None),
            P("shard", "context", None),
            P(),
            P(("shard", "context"), None, "tensor"),
            P(("shard", "context"), None),
            P(("shard", "context"), "tensor"),
            P(None, "tensor"),
            P(),
            P("tensor"),
            P("tensor"),
            P("tensor"),
            P("tensor"),
            P("tensor", ("shard", "context")),
            P(),
            P(),
        ),
        check_vma=False,
    )
```

profile of v0, /device:TPU:0, one launch (start us, length us, event | category | flops | bytes accessed | tf_op | source)
XLA Modules:
  0.0 1050.1 jit_solution(12844477060453908155)
XLA Ops:
  8.8 2.7 fusion.14
  12.1 15.0 %all_gather.34 = bf16[1536,12]{0,1:T(8,128)(2,1)S(1)} all-gather(bf16[384,12]{0,1:T(8,128)(2,1)S(1)} %copy-done.75), channel_id=1, replica_groups=mesh['shard'=4,'context'=2,'tensor'=4] {'shard'}, dimensions={0}, use_global_device_ids=true | all-gather | bytes 46080 | tf_op jit(solution)/shard_map/all_gather | solution.py:96
  32.2 29.5 %all_gather.33 = bf16[1536,256]{1,0:T(8,128)(2,1)S(1)} all-gather(bf16[384,256]{1,0:T(8,128)(2,1)} %param.24), channel_id=1, replica_groups=mesh['shard'=4,'context'=2,'tensor'=4] {'shard'}, dimensions={0}, use_global_device_ids=true | all-gather | bytes 983040 | tf_op jit(solution)/shard_map/all_gather | solution.py:95
  68.2 46.2 %all-gather.6.cloned.1.call-done = bf16[1536,2,768]{2,1,0:T(2,128)(2,1)} async-done(((bf16[384,2,768]{2,1,0:T(2,128)(2,1)}), bf16[1536,2,768]{2,1,0:T(2,128)(2,1)}) %all-gather.6.cloned.1.call-update) | async-done | bytes 4718608 | tf_op jit(solution)/shard_map/all_gather | solution.py:94
  114.4 3.4 copy.488
  117.8 5.1 fusion.61
  129.0 3.4 collective-permute-start
  140.0 5.4 all-reduce
  151.0 10.0 multiply_convert_fusion.3
  161.0 2.9 fusion.125
  164.7 2.7 copy.402
  167.4 3.9 reshape.673
  171.3 3.1 convolution_bitcast_fusion
  176.4 12.2 %while.60 = (s32[]{:T(128)}, f32[1,12,128,64]{3,2,1,0:T(8,128)S(1)}, f32[4,1,12,128,64]{4,3,2,1,0:T(8,128)}, f32[4,1,12]{2,1,0:T(1,128)}, f32[4,1,12,128,64]{3,4,2,0,1:T(8,128)}, /*index=5*/s32[]{:T(128)}, s32[]{:T(128)}) while((s32[]{:T(128)}, f32[1,12,128,64]{3,2,1,0:T(8,128)S(1)}, f32[4,1,12,128,64]{4,3,2,1,0:T(8,128)}, ...), condition=%wide.region_4.5_spmd.clone, body=%wide.region_3.4_spmd.clone.sunk | while | flops 393219 | bytes 3932912 | solution.py:154
  192.9 3.6 copy.426
  196.5 5.2 reshape.700
  201.7 10.5 %all-gather.1 = f32[2,12,128,64]{2,3,1,0:T(8,128)} all-gather(f32[1,12,128,64]{2,3,1,0:T(8,128)S(1)} %copy.421), channel_id=3, replica_groups=mesh['shard'=4,'context'=2,'tensor'=4] {'context'}, dimensions={0}, use_global_device_ids=true | all-gather | bytes 1179648 | tf_op jit(solution)/shard_map/all_gather | solution.py:19
  212.2 6.7 fusion.32
  218.9 4.3 while.61
  223.2 6.2 bitcast_add_fusion.5
  231.5 2.4 copy.489
  233.9 3.6 copy.429
  237.5 5.4 multiply_reduce_fusion.10
  242.9 5.6 psum.91
  248.5 8.6 multiply_reduce_fusion.8
  257.1 6.7 psum.93
  263.9 8.0 fusion.52
  271.9 2.6 copy.431
  274.5 3.2 copy.433
  277.7 3.9 reshape.688
  281.5 4.4 fusion.73
  288.0 12.2 %while.62 = (s32[]{:T(128)}, f32[1,12,128,64]{3,2,1,0:T(8,128)S(1)}, f32[4,1,12,128,64]{4,3,2,1,0:T(8,128)}, f32[4,1,12,128,64]{3,4,2,0,1:T(8,128)}, f32[4,1,12]...) while((s32[]{:T(128)}, f32[1,12,128,64]{3,2,1,0:T(8,128)S(1)}, ...), condition=%wide.region_15.16_spmd.clone, body=%wide.region_14.15_spmd.clone.sunk | while | flops 393220 | bytes 3932424 | solution.py:221
  300.5 10.7 %all-gather.2 = f32[2,12,128,64]{2,3,1,0:T(8,128)S(1)} all-gather(f32[1,12,128,64]{2,3,1,0:T(8,128)S(1)} %copy.438), channel_id=4, replica_groups=mesh['shard'=4,'context'=2,'tensor'=4] {'context'}, dimensions={0}, use_global_device_ids=true | all-gather | bytes 1179648 | tf_op jit(solution)/shard_map/all_gather | solution.py:19
  313.5 3.5 fusion.55
  318.9 4.0 fusion.77
  323.0 11.9 %fusion.12 = (f32[4,12,256]{2,1,0:T(8,128)}, f32[4,12,256]{2,1,0:T(8,128)}, f32[4,12,256]{2,1,0:T(8,128)}, f32[4,256,256]{2,1,0:T(8,128)}) fusion(f32[4,12,256]{2,1,0:T(8,128)S(1)} %copy-done.61, f32[256,256]{1,0:T(8,128)S(1)} %copy-done.46, f32[4,12,256]{2,1,0:T(8,128)S(1)} %copy-done.59, f32[4,256,256]{2,1,0:T(8,128)S(1)} %copy-done.33, ...), kind=kOutput, calls=%fused_computation.32 | convolution fusion | flops 446394368 | bytes 5816320 | tf_op jit(solution)/shard_map/scihp,scjhp->schij/dot_general | solution.py:198
  335.1 3.9 fusion.54
  340.8 2.4 fusion.26
  349.4 5.1 reduce-window.16
  357.5 2.9 reshape.701
  360.4 7.3 fusion.51
  369.8 3.0 reshape.689
  372.8 3.7 copy.451
  390.7 25.7 %all-reduce.6.cloned.1.call-done = f32[1,1024,256]{2,1,0:T(8,128)} async-done(((f32[1,1024,256]{2,1,0:T(8,128)}), f32[1,1024,256]{2,1,0:T(8,128)}) %all-reduce.6.cloned.1.call-update) | async-done | bytes 1048592 | tf_op jit(solution)/shard_map/psum | solution.py:258
  416.4 11.7 %fusion.119 = (f32[1024]{0:T(1024)S(1)}, f32[1024]{0:T(1024)S(1)}, f32[1024]{0:T(1024)S(1)}, f32[1024]{0:T(1024)S(1)}, f32[1024]{0:T(1024)S(1)}, /*index=5*/f32[1,1024,1024]{2,1,0:T(8,128)S(1)}) fusion(f32[1024,256]{1,0:T(8,128)} %fusion.129, f32[1024,768]{1,0:T(8,128)} %copy-done.9, f32[1,1024,1024]{2,1,0:T(8,128)} %copy-done.7, ...), kind=kLoop, calls=%fused_computation.207 | loop fusion | flops 23063552 | bytes 21004288 | tf_op jit(solution)/shard_map/reduce_sum | solution.py:277
  429.7 5.1 fusion.118
  440.4 5.1 fusion.70
  445.5 3.7 convolution_add_fusion.1
  449.3 3.8 fusion.69
  453.1 4.7 copy.481
  457.8 10.5 fusion.49
  468.3 3.2 fusion.92
  471.8 7.7 fusion.56
  480.4 2.8 reduce-scatter.13.cloned.1.call-done
  484.9 221.3 %all-reduce.8.cloned.1.call-done = (f32[1024,1536]{1,0:T(8,128)}, f32[1024,1536]{1,0:T(8,128)}) async-done(((f32[1024,1536]{1,0:T(8,128)}, f32[1024,1536]{1,0:T(8,128)}), (f32[1024,1536]{1,0:T(8,128)}, f32[1024,1536]{1,0:T(8,128)})) %all-reduce.8.cloned.1.call-update) | async-done | bytes 12582928 | tf_op jit(solution)/shard_map/psum | solution.py:181
  706.1 4.3 convolution_add_fusion
  710.5 2.9 copy-done.18
  713.4 5.9 multiply_reduce_fusion.3
  720.7 41.1 %all-reduce.1 = (f32[1536]{0:T(1024)}, f32[5,768]{1,0:T(8,128)}, f32[5,256]{1,0:T(8,128)}, f32[12]{0:T(128)}, f32[12]{0:T(128)}, /*index=5*/f32[12]{0:T(128)}, f32[768]{0:T(1024)}, f32[2]{0:T(128)S(1)}) all-reduce(f32[1536]{0:T(1024)S(1)} %get-tuple-element.717, ...), channel_id=1, replica_groups=mesh['shard'=4,'context'=2,'tensor'=4] {'shard','context'}, use_global_device_ids=true, to_apply=%region_34.35 | all-reduce | flops 7462 | bytes 59696 | tf_op jit(solution)/shard_map/psum | solution.py:296
  763.8 6.4 fusion.19
  770.2 103.1 %reduce-scatter.7.cloned.1.call-done = f32[192,2,768]{2,0,1:T(8,128)} async-done(((f32[1536,2,768]{2,0,1:T(8,128)}), f32[192,2,768]{2,0,1:T(8,128)}) %reduce-scatter.7.cloned.1.call-update) | async-done | bytes 1179664 | tf_op jit(solution)/shard_map/reduce_scatter | solution.py:310
  873.2 3.2 copy.469
  876.4 65.6 %reduce-scatter.9.cloned.1.call-done = f32[192,256]{1,0:T(8,128)} async-done(((f32[1536,256]{1,0:T(8,128)}), f32[192,256]{1,0:T(8,128)}) %reduce-scatter.9.cloned.1.call-update) | async-done | bytes 196624 | tf_op jit(solution)/shard_map/reduce_scatter | solution.py:311
  942.1 98.7 %reduce-scatter.11.cloned.1.call-done = f32[768,192]{0,1:T(8,128)} async-done(((f32[768,1536]{0,1:T(8,128)}), f32[768,192]{0,1:T(8,128)}) %reduce-scatter.11.cloned.1.call-update) | async-done | bytes 589840 | tf_op jit(solution)/shard_map/reduce_scatter | solution.py:188
  (360 shorter events, 117.4 us)
Async XLA Ops:
  7.2 4.9 copy-start.75
  7.2 19.9 %copy-start.85 = (f32[12]{0:T(128)S(1)}, f32[12]{0:T(128)}, u32[]{:S(2)}) copy-start(f32[12]{0:T(128)} %param.29) | copy-start | bytes 148
  7.2 19.9 %copy-start.50 = (f32[1536]{0:T(1024)S(1)}, f32[1536]{0:T(1024)}, u32[]{:S(2)}) copy-start(f32[1536]{0:T(1024)} %param.22) | copy-start | bytes 18436
  7.2 107.2 %all-gather.6.cloned.1.call-start = ((), (), s32[]{:S(2)}) async-start(), calls=%async_computation.4 | async-start | bytes 5898240 | tf_op jit(solution)/shard_map/all_gather | solution.py:94
  7.9 240.6 %all-gather.8.cloned.1.call-start = ((), (), s32[]{:S(2)}) async-start(), calls=%async_computation.5 | async-start | bytes 2949120 | tf_op jit(solution)/shard_map/all_gather | solution.py:97
  8.7 407.7 %all-reduce.6.cloned.1.call-start = ((), (), s32[]{:S(2)}) async-start(), calls=%async_computation.6 | async-start | bytes 2097152 | tf_op jit(solution)/shard_map/psum | solution.py:258
  8.7 18.4 %copy-start.3 = (bf16[1,1024,1536]{2,1,0:T(8,128)(2,1)S(1)}, bf16[1,1024,1536]{2,1,0:T(8,128)(2,1)}, u32[]{:S(2)}) copy-start(bf16[1,1024,1536]{2,1,0:T(8,128)(2,1)} %param.21) | copy-start | bytes 9437188
  12.1 105.7 %copy-start.62 = (f32[1024]{0:T(1024)}, f32[1024]{0:T(1024)S(1)}, u32[]{:S(2)}) copy-start(f32[1024]{0:T(1024)S(1)} %get-tuple-element.803) | copy-start | bytes 12292
  28.0 33.7 %copy-start.1 = (bf16[1024,1536]{1,0:T(8,128)(2,1)}, bf16[1024,1536]{1,0:T(8,128)(2,1)S(1)}, u32[]{:S(2)}) copy-start(bf16[1024,1536]{1,0:T(8,128)(2,1)S(1)} %fusion.16) | copy-start | bytes 9437188
  29.7 34.0 %copy-start.40 = (f32[1,4,256,12]{2,1,3,0:T(4,128)}, f32[1,4,256,12]{2,1,3,0:T(4,128)S(1)}, u32[]{:S(2)}) copy-start(f32[1,4,256,12]{2,1,3,0:T(4,128)S(1)} %reshape.676) | copy-start | bytes 147460
  65.4 52.4 %copy-start.31 = (f32[1,4,256,12]{2,1,3,0:T(4,128)}, f32[1,4,256,12]{2,1,3,0:T(4,128)S(1)}, u32[]{:S(2)}) copy-start(f32[1,4,256,12]{2,1,3,0:T(4,128)S(1)} %get-tuple-element.778) | copy-start | bytes 147460
  66.8 82.1 %copy-start.34 = (f32[1,4,256,12]{2,1,3,0:T(4,128)}, f32[1,4,256,12]{2,1,3,0:T(4,128)S(1)}, u32[]{:S(2)}) copy-start(f32[1,4,256,12]{2,1,3,0:T(4,128)S(1)} %reshape.682) | copy-start | bytes 147460
  117.8 5.1 copy-start.23
  129.0 22.0 %collective-permute-start = (f32[1,3,1024]{2,1,0:T(4,128)}, f32[1,3,1024]{2,1,0:T(4,128)S(1)}, u32[]{:S(2)}, u32[]{:S(2)}) collective-permute-start(f32[1,3,1024]{2,1,0:T(4,128)} %slice.128), channel_id=1, source_target_pairs={{0,4},{1,5},{2,6},{3,7},{8,12},{9,13},{10,14},{11,15},{16,20},{17,... | collective-permute-start | bytes 36872 | tf_op jit(solution)/shard_map/ppermute | solution.py:14
  151.0 10.0 copy-start.64
  164.6 6.6 copy-start.25
  164.7 6.6 copy-start.56
  196.5 15.7 %copy-start.45 = (f32[256,256]{1,0:T(8,128)S(1)}, f32[256,256]{1,0:T(8,128)}, u32[]{:S(2)}) copy-start(f32[256,256]{1,0:T(8,128)} %get-tuple-element.813) | copy-start | bytes 786436
  196.5 15.7 %copy-start.52 = (pred[256,256]{1,0:T(8,128)(4,1)S(1)}, pred[256,256]{1,0:T(8,128)(4,1)}, u32[]{:S(2)}) copy-start(pred[256,256]{1,0:T(8,128)(4,1)} %get-tuple-element.812) | copy-start | bytes 196612
  196.5 15.7 %copy-start.58 = (f32[4,12,256]{2,1,0:T(8,128)S(1)}, f32[4,12,256]{2,1,0:T(8,128)}, u32[]{:S(2)}) copy-start(f32[4,12,256]{2,1,0:T(8,128)} %copy.408) | copy-start | bytes 147460
  196.5 15.7 %copy-start.60 = (f32[4,12,256]{2,1,0:T(8,128)S(1)}, f32[4,12,256]{2,1,0:T(8,128)}, u32[]{:S(2)}) copy-start(f32[4,12,256]{2,1,0:T(8,128)} %copy.410) | copy-start | bytes 147460
  212.2 6.7 copy-start.6
  237.5 11.1 %copy-start.80 = (f32[768]{0:T(1024)S(1)}, f32[768]{0:T(1024)}, u32[]{:S(2)}) copy-start(f32[768]{0:T(1024)} %param.31) | copy-start | bytes 9220
  248.5 15.4 %copy-start.72 = (f32[1024]{0:T(1024)}, f32[1024]{0:T(1024)S(1)}, u32[]{:S(2)}) copy-start(f32[1024]{0:T(1024)S(1)} %get-tuple-element.805) | copy-start | bytes 12292
  274.5 7.0 copy-start.28
  274.5 7.0 copy-start.43
  313.5 5.3 copy-start.57
  323.0 11.9 %copy-start.17 = (bf16[1,1024,128]{2,1,0:T(8,128)(2,1)S(1)}, bf16[1,1024,128]{2,1,0:T(8,128)(2,1)}, u32[]{:S(2)}) copy-start(bf16[1,1024,128]{2,1,0:T(8,128)(2,1)} %get-tuple-element.788) | copy-start | bytes 786436
  323.0 12.0 %copy-start.69 = (f32[4,12]{1,0:T(4,128)S(1)}, f32[4,12]{1,0:T(4,128)}, u32[]{:S(2)}) copy-start(f32[4,12]{1,0:T(4,128)} %get-tuple-element.806) | copy-start | bytes 580
  323.0 12.0 %copy-start.70 = (f32[4,12]{1,0:T(4,128)S(1)}, f32[4,12]{1,0:T(4,128)}, u32[]{:S(2)}) copy-start(f32[4,12]{1,0:T(4,128)} %get-tuple-element.807) | copy-start | bytes 580
  343.3 14.2 %copy-start.12 = (f32[1024,768]{0,1:T(8,128)S(1)}, f32[1024,768]{0,1:T(8,128)}, u32[]{:S(2)}) copy-start(f32[1024,768]{0,1:T(8,128)} %copy.433) | copy-start | bytes 9437188
  372.8 4.7 copy-start.24
  372.8 4.7 copy-start.37
  378.6 6.6 copy-start.47
  378.6 7.7 copy-start.48
  378.6 8.7 copy-start.41
  378.6 8.7 copy-start.78
  378.6 9.9 copy-start.42
  378.6 10.0 copy-start.2
  381.9 101.3 %reduce-scatter.13.cloned.1.call-start = ((), (), s32[]{:S(2)}) async-start(), calls=%async_computation.10 | async-start | bytes 884736
  388.7 27.8 %copy-start.65 = (f32[1,3,1024]{2,1,0:T(4,128)S(1)}, f32[1,3,1024]{2,1,0:T(4,128)}, u32[]{:S(2)}) copy-start(f32[1,3,1024]{2,1,0:T(4,128)} %copy-done.64) | copy-start | bytes 36868
  390.6 315.5 %all-reduce.8.cloned.1.call-start = ((), (), s32[]{:S(2)}) async-start(), calls=%async_computation.11 | async-start | bytes 25165824 | tf_op jit(solution)/shard_map/psum | solution.py:181
  416.4 13.3 %copy-start.14 = (f32[1024,768]{1,0:T(8,128)S(1)}, f32[1024,768]{1,0:T(8,128)}, u32[]{:S(2)}) copy-start(f32[1024,768]{1,0:T(8,128)} %get-tuple-element.776) | copy-start | bytes 9437188
  416.4 13.3 %copy-start.73 = (f32[1024]{0:T(1024)S(1)}, f32[1024]{0:T(1024)}, u32[]{:S(2)}) copy-start(f32[1024]{0:T(1024)} %copy-done.72) | copy-start | bytes 12292
  416.4 13.3 %copy-start.81 = (f32[768]{0:T(1024)S(1)}, f32[768]{0:T(1024)}, u32[]{:S(2)}) copy-start(f32[768]{0:T(1024)} %param.31) | copy-start | bytes 9220
  416.4 13.3 %copy-start.84 = (bf16[768,1536]{1,0:T(8,128)(2,1)S(1)}, bf16[768,1536]{1,0:T(8,128)(2,1)}, u32[]{:S(2)}) copy-start(bf16[768,1536]{1,0:T(8,128)(2,1)} %all-gather.8.cloned.1.call-done) | copy-start | bytes 7077892
  416.4 22.2 %slice-start = ((s8[4718592]{0:T(1024)(128)(4,1)}), s8[4194304]{0:T(1024)(128)(4,1)S(1)}, s32[]{:S(2)}) async-start(s8[4718592]{0:T(1024)(128)(4,1)} %bitcast.347), calls=%async_computation.12 | async-start | bytes 8388608
  428.2 6.6 copy-start.66
  428.2 6.6 copy-start.67
  428.2 10.4 slice-start.1
  428.2 6.6 collective-permute-start.1
  438.6 6.9 copy-start.21
  440.4 5.1 copy-start.39
  449.2 424.0 %reduce-scatter.7.cloned.1.call-start = ((), (), s32[]{:S(2)}) async-start(), calls=%async_computation.7 | async-start | bytes 10616832 | tf_op jit(solution)/shard_map/reduce_scatter | solution.py:310
  453.1 4.7 copy-start.63
  468.3 473.8 %reduce-scatter.9.cloned.1.call-start = ((), (), s32[]{:S(2)}) async-start(), calls=%async_computation.8 | async-start | bytes 1769472 | tf_op jit(solution)/shard_map/reduce_scatter | solution.py:311
  471.5 569.3 %reduce-scatter.11.cloned.1.call-start = ((), (), s32[]{:S(2)}) async-start(), calls=%async_computation.9 | async-start | bytes 5308416 | tf_op jit(solution)/shard_map/reduce_scatter | solution.py:188
  484.8 225.6 %copy-start.49 = (f32[5,1024]{1,0:T(8,128)}, f32[5,1024]{1,0:T(8,128)S(1)}, u32[]{:S(2)}) copy-start(f32[5,1024]{1,0:T(8,128)S(1)} %stack.32) | copy-start | bytes 61444
  706.1 7.3 copy-start.18
  710.5 8.8 copy-start
  713.4 7.3 slice-start.2
  713.4 7.3 slice-start.3
  713.4 7.3 copy-start.79
  713.4 50.4 %copy-start.71 = (f32[1024]{0:T(1024)S(1)}, f32[1024]{0:T(1024)}, u32[]{:S(2)}) copy-start(f32[1024]{0:T(1024)} %get-tuple-element.802) | copy-start | bytes 12292
  (36 other events, 96.9 us)
Sparse Core Ops, SparseCore 0:
  9.6 104.7 all-gather.5
  116.0 48.6 all-gather.7
  382.0 34.3 all-reduce.5
  419.6 63.6 reduce-scatter.12
  486.2 219.8 all-reduce.7
  709.6 163.6 reduce-scatter.6
  877.2 64.8 reduce-scatter.8
  946.3 94.4 reduce-scatter.10
where the time goes:
time: 1060 us; the launch traced here: 1050 us
  waiting for transfers between devices  565 us (53%)
  local copies, waits for them, and re-layouts  125 us (12%)
  blocking collectives  125 us (12%)
  matrix products  111 us (10%)
  other arithmetic  99.2 us (9%)
  between operations  19.7 us (2%)
    psum x1, waiting for transfers between devices, on_device(): lax.psum(jnp.dot(out_in, out_full, preferred_element_type=jnp.float32), '...  221 us
    reduce_scatter x1, waiting for transfers between devices, on_device(): lax.psum_scatter(grad_wzx, ('shard', 'context'), scatter_dimension=0, til...  103 us
    reduce_scatter x1, waiting for transfers between devices, on_device(): lax.psum_scatter(grad_wout, ('shard', 'context'), scatter_dimension=1, ti...  98.7 us
    reduce_scatter x1, waiting for transfers between devices, on_device(): lax.psum_scatter(grad_wbc, ('shard', 'context'), scatter_dimension=0, til...  65.6 us
    all_gather x1, waiting for transfers between devices, on_device(): lax.all_gather(w_in_zx, 'shard', axis=0, tiled=True)  46.2 us
    psum x1, blocking collectives, on_device(): lax.psum((grad_ng, grad_taps[:, :inner_dev], grad_taps[:, inner_dev:], gr...  41.1 us
    all_gather x1, blocking collectives, on_device(): lax.all_gather(w_in_bc, 'shard', axis=0, tiled=True)  29.5 us
    psum x1, waiting for transfers between devices, on_device(): bc_sum = lax.psum(bc_part, 'tensor')  25.7 us
  transfers between devices with their start and end apart: 10, of which 7 were waited for; matrix products, arithmetic and copies ran while one was open for 20% of the time, Pallas kernels for 0%

commit v1 on v0

--- a/solution.py
+++ b/solution.py
@@ -255,7 +255,9 @@
     grad_raw = grad_dt_q.reshape(row_count, heads_dev) * jax.nn.sigmoid(dt_pre)
     grad_dtb = jnp.sum(grad_raw, axis=0)
     bc_part = jnp.concatenate([grad_bm, grad_cm], axis=-1).reshape(row_count, 2 * state_dim)
-    bc_sum = lax.psum(bc_part, "tensor")
+    bc_sum = bc_part
+    for hop_ in (1, 2):
+        bc_sum = bc_sum + lax.ppermute(bc_sum, "tensor", [(dev, dev ^ hop_) for dev in range(4)])
     grad_act = jnp.concatenate(
         [
             grad_xa.reshape(seq_count, local_len, inner_dev),

time: 1060 us -> 1020 us (0.962)
  waiting for transfers between devices: 565 us -> 529 us
    psum x1 -> x0, waiting for transfers between devices: 25.7 us -> none  [on_device(): bc_sum = lax.psum(bc_part, 'tensor')]
    psum x1, waiting for transfers between devices: 221 us -> 198 us  [on_device(): lax.psum(jnp.dot(out_in, out_full, preferred_element_type=jnp.float32), '...]
    ppermute x0 -> x2, waiting for transfers between devices: none -> 19.2 us  [on_device(): lax.ppermute(bc_sum, 'tensor', [(dev, dev ^ hop_) for dev in range(4)])]
    unnamed x186 -> x188, local copies, waits for them, and re-layouts: 23.9 us -> 22.5 us
  transfers between devices with their start and end apart: 10 -> 11, of which waited for: 7 -> 6; matrix products, arithmetic and copies ran while one was open for 20% -> 22% of each run, Pallas kernels for 0% -> 0%
where the time goes in v1:
time: 1020 us; the launch traced here: 1010 us
  waiting for transfers between devices  529 us (52%)
  blocking collectives  125 us (12%)
  matrix products  118 us (12%)
  local copies, waits for them, and re-layouts  116 us (11%)
  other arithmetic  98.2 us (10%)
  between operations  19.9 us (2%)
    psum x1, waiting for transfers between devices, on_device(): lax.psum(jnp.dot(out_in, out_full, preferred_element_type=jnp.float32), '...  198 us
    reduce_scatter x1, waiting for transfers between devices, on_device(): lax.psum_scatter(grad_wzx, ('shard', 'context'), scatter_dimension=0, til...  103 us
    reduce_scatter x1, waiting for transfers between devices, on_device(): lax.psum_scatter(grad_wout, ('shard', 'context'), scatter_dimension=1, ti...  98.7 us
    reduce_scatter x1, waiting for transfers between devices, on_device(): lax.psum_scatter(grad_wbc, ('shard', 'context'), scatter_dimension=0, til...  65.4 us
    all_gather x1, waiting for transfers between devices, on_device(): lax.all_gather(w_in_zx, 'shard', axis=0, tiled=True)  43.2 us
    psum x1, blocking collectives, on_device(): lax.psum((grad_ng, grad_taps[:, :inner_dev], grad_taps[:, inner_dev:], gr...  40.9 us
    all_gather x1, blocking collectives, on_device(): lax.all_gather(w_in_bc, 'shard', axis=0, tiled=True)  30.1 us
    unnamed x188, local copies, waits for them, and re-layouts  22.5 us
  transfers between devices with their start and end apart: 11, of which 6 were waited for; matrix products, arithmetic and copies ran while one was open for 22% of the time, Pallas kernels for 0%

profile of v1, /device:TPU:0, one launch (start us, length us, event | category | flops | bytes accessed | tf_op | source)
XLA Modules:
  0.0 1014.2 jit_solution(1849182805874339387)
XLA Ops:
  8.8 2.7 fusion.14
  12.1 15.0 %all_gather.34 = bf16[1536,12]{0,1:T(8,128)(2,1)S(1)} all-gather(bf16[384,12]{0,1:T(8,128)(2,1)S(1)} %copy-done.73), channel_id=1, replica_groups=mesh['shard'=4,'context'=2,'tensor'=4] {'shard'}, dimensions={0}, use_global_device_ids=true | all-gather | bytes 46080 | tf_op jit(solution)/shard_map/all_gather | solution.py:96
  33.8 30.1 %all_gather.33 = bf16[1536,256]{1,0:T(8,128)(2,1)S(1)} all-gather(bf16[384,256]{1,0:T(8,128)(2,1)S(1)} %copy-done.44), channel_id=1, replica_groups=mesh['shard'=4,'context'=2,'tensor'=4] {'shard'}, dimensions={0}, use_global_device_ids=true | all-gather | bytes 983040 | tf_op jit(solution)/shard_map/all_gather | solution.py:95
  63.9 3.2 fusion.130
  71.1 43.2 %all-gather.6.cloned.1.call-done = bf16[1536,2,768]{2,1,0:T(2,128)(2,1)} async-done(((bf16[384,2,768]{2,1,0:T(2,128)(2,1)}), bf16[1536,2,768]{2,1,0:T(2,128)(2,1)}) %all-gather.6.cloned.1.call-update) | async-done | bytes 4718608 | tf_op jit(solution)/shard_map/all_gather | solution.py:94
  114.4 3.4 copy.488
  117.9 5.1 fusion.61
  129.0 3.9 collective-permute-start
  139.3 5.4 all-reduce
  148.9 10.0 multiply_convert_fusion.3
  158.9 2.7 fusion.126
  162.5 2.7 copy.402
  165.2 3.8 reshape.673
  169.1 3.1 convolution_bitcast_fusion
  174.2 9.7 while.60
  188.3 3.6 copy.426
  191.9 5.2 reshape.700
  197.1 10.5 %all-gather.1 = f32[2,12,128,64]{2,3,1,0:T(8,128)} all-gather(f32[1,12,128,64]{2,3,1,0:T(8,128)S(1)} %copy.421), channel_id=3, replica_groups=mesh['shard'=4,'context'=2,'tensor'=4] {'context'}, dimensions={0}, use_global_device_ids=true | all-gather | bytes 1179648 | tf_op jit(solution)/shard_map/all_gather | solution.py:19
  207.6 6.7 fusion.32
  214.3 3.0 while.61
  217.3 6.0 bitcast_add_fusion.5
  227.9 3.5 copy.429
  231.4 5.4 multiply_reduce_fusion.10
  236.8 5.6 psum.84
  242.5 8.6 multiply_reduce_fusion.8
  251.0 6.7 psum.86
  257.8 7.4 fusion.52
  267.8 3.1 copy.433
  270.9 3.9 reshape.688
  274.8 4.4 fusion.73
  281.2 9.7 while.62
  291.2 10.7 %all-gather.2 = f32[2,12,128,64]{2,3,1,0:T(8,128)S(1)} all-gather(f32[1,12,128,64]{2,3,1,0:T(8,128)S(1)} %copy.438), channel_id=4, replica_groups=mesh['shard'=4,'context'=2,'tensor'=4] {'context'}, dimensions={0}, use_global_device_ids=true | all-gather | bytes 1179648 | tf_op jit(solution)/shard_map/all_gather | solution.py:19
  304.2 3.5 fusion.55
  310.2 4.0 fusion.77
  314.3 11.5 %fusion.12 = (f32[4,12,256]{2,1,0:T(8,128)}, f32[4,12,256]{2,1,0:T(8,128)}, f32[4,12,256]{2,1,0:T(8,128)}, f32[4,256,256]{2,1,0:T(8,128)S(1)}) fusion(f32[4,12,256]{2,1,0:T(8,128)S(1)} %copy-done.60, f32[256,256]{1,0:T(8,128)S(1)} %copy-done.43, f32[4,12,256]{2,1,0:T(8,128)S(1)} %copy-done.58, f32[4,256,256]{2,1,0:T(8,128)S(1)} %copy-done.31, ...), kind=kOutput, calls=%fused_computation.32 | convolution fusion | flops 446394368 | bytes 5816320 | tf_op jit(solution)/shard_map/scihp,scjhp->schij/dot_general | solution.py:198
  326.8 3.4 fusion.132
  330.2 5.2 reshape.701
  335.4 3.1 fusion.47
  339.2 7.7 fusion.51
  359.9 5.6 copy.442
  365.5 5.2 reshape.689
  370.7 3.5 copy.451
  374.3 3.8 fusion.54
  383.8 3.8 fusion.105
  387.6 19.2 %collective-permute-done.2 = f32[1024,256]{1,0:T(8,128)S(1)} collective-permute-done((f32[1024,256]{1,0:T(8,128)}, f32[1024,256]{1,0:T(8,128)S(1)}, u32[]{:S(2)}, u32[]{:S(2)}) %collective-permute-start.2) | collective-permute-done | bytes 1048608 | tf_op jit(solution)/shard_map/ppermute | solution.py:260
  408.3 11.2 %fusion.120 = (f32[1024]{0:T(1024)S(1)}, f32[1024]{0:T(1024)S(1)}, f32[1024]{0:T(1024)S(1)}, f32[1024]{0:T(1024)S(1)}, f32[1024]{0:T(1024)S(1)}, /*index=5*/f32[1,1024,1024]{2,1,0:T(8,128)S(1)}) fusion(f32[1024,256]{1,0:T(8,128)S(1)} %copy-done.14, f32[1024,768]{1,0:T(8,128)} %copy-done.8, f32[1,1024,1024]{2,1,0:T(8,128)} %copy-done.6, ...), kind=kLoop, calls=%fused_computation.209 | loop fusion | flops 23063552 | bytes 21004288 | tf_op jit(solution)/shard_map/reduce_sum | solution.py:279
  421.0 5.1 fusion.119
  430.4 5.1 fusion.70
  435.5 3.7 convolution_add_fusion.1
  439.2 3.9 fusion.69
  443.1 4.7 copy.481
  447.8 10.4 %fusion.49 = f32[1536,2,768]{2,0,1:T(8,128)} fusion(bf16[2,768,1024]{2,1,0:T(8,128)(2,1)} %bitcast.359, bf16[1,1024,1536]{2,1,0:T(8,128)(2,1)} %param.21, f32[1536]{0:T(1024)S(1)} %copy-done.49, f32[1024]{0:T(1024)S(1)} %copy-done.64), kind=kOutput, calls=%fused_computation.92 | convolution fusion | flops 4838129664 | bytes 15738880 | tf_op jit(solution)/shard_map/dot_general | solution.py:44
  458.2 4.1 fusion.92
  462.6 7.8 fusion.56
  472.3 198.1 %all-reduce.5.cloned.1.call-done = (f32[1024,1536]{1,0:T(8,128)}, f32[1024,1536]{1,0:T(8,128)}) async-done(((f32[1024,1536]{1,0:T(8,128)}, f32[1024,1536]{1,0:T(8,128)}), (f32[1024,1536]{1,0:T(8,128)}, f32[1024,1536]{1,0:T(8,128)})) %all-reduce.5.cloned.1.call-update) | async-done | bytes 12582928 | tf_op jit(solution)/shard_map/psum | solution.py:181
  670.5 4.0 convolution_add_fusion
  674.5 3.0 copy-done.16
  677.4 5.9 multiply_reduce_fusion.3
  684.7 40.9 %all-reduce.1 = (f32[1536]{0:T(1024)}, f32[5,768]{1,0:T(8,128)}, f32[5,256]{1,0:T(8,128)}, f32[12]{0:T(128)}, f32[12]{0:T(128)}, /*index=5*/f32[12]{0:T(128)}, f32[768]{0:T(1024)}, f32[2]{0:T(128)S(1)}) all-reduce(f32[1536]{0:T(1024)S(1)} %get-tuple-element.717, ...), channel_id=1, replica_groups=mesh['shard'=4,'context'=2,'tensor'=4] {'shard','context'}, use_global_device_ids=true, to_apply=%region_33.34 | all-reduce | flops 7462 | bytes 59696 | tf_op jit(solution)/shard_map/psum | solution.py:298
  727.6 7.3 fusion.19
  734.9 102.6 %reduce-scatter.7.cloned.1.call-done = f32[192,2,768]{2,0,1:T(8,128)} async-done(((f32[1536,2,768]{2,0,1:T(8,128)}), f32[192,2,768]{2,0,1:T(8,128)}) %reduce-scatter.7.cloned.1.call-update) | async-done | bytes 1179664 | tf_op jit(solution)/shard_map/reduce_scatter | solution.py:312
  837.6 3.2 copy.469
  840.8 65.4 %reduce-scatter.9.cloned.1.call-done = f32[192,256]{1,0:T(8,128)} async-done(((f32[1536,256]{1,0:T(8,128)}), f32[192,256]{1,0:T(8,128)}) %reduce-scatter.9.cloned.1.call-update) | async-done | bytes 196624 | tf_op jit(solution)/shard_map/reduce_scatter | solution.py:313
  906.2 98.7 %reduce-scatter.11.cloned.1.call-done = f32[768,192]{0,1:T(8,128)} async-done(((f32[768,1536]{0,1:T(8,128)}), f32[768,192]{0,1:T(8,128)}) %reduce-scatter.11.cloned.1.call-update) | async-done | bytes 589840 | tf_op jit(solution)/shard_map/reduce_scatter | solution.py:188
  (365 shorter events, 105.7 us)
Async XLA Ops:
  7.2 19.9 %copy-start.85 = (f32[12]{0:T(128)S(1)}, f32[12]{0:T(128)}, u32[]{:S(2)}) copy-start(f32[12]{0:T(128)} %param.29) | copy-start | bytes 148
  7.2 19.9 %copy-start.48 = (f32[1536]{0:T(1024)S(1)}, f32[1536]{0:T(1024)}, u32[]{:S(2)}) copy-start(f32[1536]{0:T(1024)} %param.22) | copy-start | bytes 18436
  7.2 107.2 %all-gather.6.cloned.1.call-start = ((), (), s32[]{:S(2)}) async-start(), calls=%async_computation.4 | async-start | bytes 5898240 | tf_op jit(solution)/shard_map/all_gather | solution.py:94
  7.9 234.5 %all-gather.8.cloned.1.call-start = ((), (), s32[]{:S(2)}) async-start(), calls=%async_computation.5 | async-start | bytes 2949120 | tf_op jit(solution)/shard_map/all_gather | solution.py:97
  8.7 462.0 %reduce-scatter.13.cloned.1.call-start = ((), (), s32[]{:S(2)}) async-start(), calls=%async_computation.9 | async-start | bytes 884736
  8.7 18.4 %copy-start.2 = (bf16[1,1024,1536]{2,1,0:T(8,128)(2,1)S(1)}, bf16[1,1024,1536]{2,1,0:T(8,128)(2,1)}, u32[]{:S(2)}) copy-start(bf16[1,1024,1536]{2,1,0:T(8,128)(2,1)} %param.21) | copy-start | bytes 9437188
  12.1 105.8 %copy-start.63 = (f32[1024]{0:T(1024)}, f32[1024]{0:T(1024)S(1)}, u32[]{:S(2)}) copy-start(f32[1024]{0:T(1024)S(1)} %get-tuple-element.803) | copy-start | bytes 12292
  67.1 81.8 %copy-start.13 = (f32[1024,256]{1,0:T(8,128)}, f32[1024,256]{1,0:T(8,128)S(1)}, u32[]{:S(2)}) copy-start(f32[1024,256]{1,0:T(8,128)S(1)} %fusion.130) | copy-start | bytes 3145732
  68.9 48.9 %copy-start.29 = (f32[1,4,256,12]{2,1,3,0:T(4,128)}, f32[1,4,256,12]{2,1,3,0:T(4,128)S(1)}, u32[]{:S(2)}) copy-start(f32[1,4,256,12]{2,1,3,0:T(4,128)S(1)} %get-tuple-element.778) | copy-start | bytes 147460
  70.4 47.5 %copy-start.45 = (f32[4,12]{0,1:T(8,128)}, f32[4,12]{0,1:T(8,128)S(1)}, u32[]{:S(2)}) copy-start(f32[4,12]{0,1:T(8,128)S(1)} %copy.417) | copy-start | bytes 580
  70.4 76.4 %copy-start.32 = (f32[1,4,256,12]{2,1,3,0:T(4,128)}, f32[1,4,256,12]{2,1,3,0:T(4,128)S(1)}, u32[]{:S(2)}) copy-start(f32[1,4,256,12]{2,1,3,0:T(4,128)S(1)} %reshape.682) | copy-start | bytes 147460
  129.0 19.9 %collective-permute-start = (f32[1,3,1024]{2,1,0:T(4,128)}, f32[1,3,1024]{2,1,0:T(4,128)}, u32[]{:S(2)}, u32[]{:S(2)}) collective-permute-start(f32[1,3,1024]{2,1,0:T(4,128)} %slice.128), channel_id=1, source_target_pairs={{0,4},{1,5},{2,6},{3,7},{8,12},{9,13},{10,14},{11,15},{16,20},{17,... | collective-permute-start | bytes 36872 | tf_op jit(solution)/shard_map/ppermute | solution.py:14
  162.5 6.6 copy-start.22
  162.5 6.6 copy-start.55
  191.8 15.7 %copy-start.42 = (f32[256,256]{1,0:T(8,128)S(1)}, f32[256,256]{1,0:T(8,128)}, u32[]{:S(2)}) copy-start(f32[256,256]{1,0:T(8,128)} %get-tuple-element.813) | copy-start | bytes 786436
  191.8 15.7 %copy-start.50 = (pred[256,256]{1,0:T(8,128)(4,1)S(1)}, pred[256,256]{1,0:T(8,128)(4,1)}, u32[]{:S(2)}) copy-start(pred[256,256]{1,0:T(8,128)(4,1)} %get-tuple-element.812) | copy-start | bytes 196612
  191.8 15.7 %copy-start.57 = (f32[4,12,256]{2,1,0:T(8,128)S(1)}, f32[4,12,256]{2,1,0:T(8,128)}, u32[]{:S(2)}) copy-start(f32[4,12,256]{2,1,0:T(8,128)} %copy.408) | copy-start | bytes 147460
  191.9 15.7 %copy-start.59 = (f32[4,12,256]{2,1,0:T(8,128)S(1)}, f32[4,12,256]{2,1,0:T(8,128)}, u32[]{:S(2)}) copy-start(f32[4,12,256]{2,1,0:T(8,128)} %copy.410) | copy-start | bytes 147460
  207.6 6.7 copy-start.5
  207.6 6.7 copy-start.86
  231.4 11.0 %copy-start.78 = (f32[768]{0:T(1024)S(1)}, f32[768]{0:T(1024)}, u32[]{:S(2)}) copy-start(f32[768]{0:T(1024)} %param.31) | copy-start | bytes 9220
  267.8 7.0 copy-start.26
  267.8 7.0 copy-start.40
  304.2 5.9 copy-start.56
  314.3 11.5 %copy-start.15 = (bf16[1,1024,128]{2,1,0:T(8,128)(2,1)S(1)}, bf16[1,1024,128]{2,1,0:T(8,128)(2,1)}, u32[]{:S(2)}) copy-start(bf16[1,1024,128]{2,1,0:T(8,128)(2,1)} %get-tuple-element.788) | copy-start | bytes 786436
  314.3 12.6 %copy-start.23 = (bf16[1,1024,128]{2,1,0:T(8,128)(2,1)S(1)}, bf16[1,1024,128]{2,1,0:T(8,128)(2,1)}, u32[]{:S(2)}) copy-start(bf16[1,1024,128]{2,1,0:T(8,128)(2,1)} %copy-done.22) | copy-start | bytes 786436
  325.8 25.6 %copy-start.21 = (f32[4,256,256]{2,1,0:T(8,128)}, f32[4,256,256]{2,1,0:T(8,128)S(1)}, u32[]{:S(2)}) copy-start(f32[4,256,256]{2,1,0:T(8,128)S(1)} %get-tuple-element.699) | copy-start | bytes 3145732
  339.2 7.7 copy-start.7
  339.2 7.7 copy-start.34
  339.2 7.7 copy-start.41
  351.4 5.3 copy-start.53
  351.4 5.3 copy-start.54
  351.4 5.3 copy-start.30
  351.4 5.3 copy-start.33
  351.4 5.3 copy-start.46
  351.4 5.3 copy-start.62
  356.7 22.1 %collective-permute-start.1 = (f32[1024,256]{1,0:T(8,128)}, f32[1024,256]{1,0:T(8,128)}, u32[]{:S(2)}, u32[]{:S(2)}) collective-permute-start(f32[1024,256]{1,0:T(8,128)} %pad_maximum_fusion.4), channel_id=1, source_target_pairs={{0,1},{1,0},{2,3},{3,2},{4,5},{5,4},{6,7},{7,6},{8,9},{9,8},{10,11... | collective-permute-start | bytes 3145736 | tf_op jit(solution)/shard_map/ppermute | solution.py:260
  378.0 5.3 copy-start.76
  378.0 5.6 copy-start.39
  381.1 25.8 %collective-permute-start.2 = (f32[1024,256]{1,0:T(8,128)}, f32[1024,256]{1,0:T(8,128)S(1)}, u32[]{:S(2)}, u32[]{:S(2)}) collective-permute-start(f32[1024,256]{1,0:T(8,128)} %fusion.118), channel_id=1, source_target_pairs={{0,2},{1,3},{2,0},{3,1},{4,6},{5,7},{6,4},{7,5},{8,10},{9,11},{10,... | collective-permute-start | bytes 3145736 | tf_op jit(solution)/shard_map/ppermute | solution.py:260
  387.6 20.7 %copy-start.14 = (f32[1024,256]{1,0:T(8,128)S(1)}, f32[1024,256]{1,0:T(8,128)}, u32[]{:S(2)}) copy-start(f32[1024,256]{1,0:T(8,128)} %copy-done.13) | copy-start | bytes 3145732
  387.6 282.9 %all-reduce.5.cloned.1.call-start = ((), (), s32[]{:S(2)}) async-start(), calls=%async_computation.10 | async-start | bytes 25165824 | tf_op jit(solution)/shard_map/psum | solution.py:181
  408.2 12.7 %copy-start.12 = (f32[1024,768]{1,0:T(8,128)S(1)}, f32[1024,768]{1,0:T(8,128)}, u32[]{:S(2)}) copy-start(f32[1024,768]{1,0:T(8,128)} %get-tuple-element.776) | copy-start | bytes 9437188
  408.2 12.7 %copy-start.79 = (f32[768]{0:T(1024)S(1)}, f32[768]{0:T(1024)}, u32[]{:S(2)}) copy-start(f32[768]{0:T(1024)} %param.31) | copy-start | bytes 9220
  408.2 12.7 %copy-start.84 = (bf16[768,1536]{1,0:T(8,128)(2,1)S(1)}, bf16[768,1536]{1,0:T(8,128)(2,1)}, u32[]{:S(2)}) copy-start(bf16[768,1536]{1,0:T(8,128)(2,1)} %all-gather.8.cloned.1.call-done) | copy-start | bytes 7077892
  408.3 20.3 %slice-start = ((s8[4718592]{0:T(1024)(128)(4,1)}), s8[4194304]{0:T(1024)(128)(4,1)S(1)}, s32[]{:S(2)}) async-start(s8[4718592]{0:T(1024)(128)(4,1)} %bitcast.347), calls=%async_computation.11 | async-start | bytes 8388608
  419.4 6.6 copy-start.65
  419.5 6.6 copy-start.66
  419.5 6.6 copy-start.67
  419.5 6.6 copy-start.68
  419.5 9.1 slice-start.1
  419.5 6.6 collective-permute-start.3
  428.6 6.9 copy-start.18
  439.2 398.4 %reduce-scatter.7.cloned.1.call-start = ((), (), s32[]{:S(2)}) async-start(), calls=%async_computation.6 | async-start | bytes 10616832 | tf_op jit(solution)/shard_map/reduce_scatter | solution.py:312
  458.2 448.0 %reduce-scatter.9.cloned.1.call-start = ((), (), s32[]{:S(2)}) async-start(), calls=%async_computation.7 | async-start | bytes 1769472 | tf_op jit(solution)/shard_map/reduce_scatter | solution.py:313
  462.4 542.5 %reduce-scatter.11.cloned.1.call-start = ((), (), s32[]{:S(2)}) async-start(), calls=%async_computation.8 | async-start | bytes 5308416 | tf_op jit(solution)/shard_map/reduce_scatter | solution.py:188
  470.4 200.0 %copy-start.25 = (bf16[1536,256]{1,0:T(8,128)(2,1)S(1)}, bf16[1536,256]{1,0:T(8,128)(2,1)}, u32[]{:S(2)}) copy-start(bf16[1536,256]{1,0:T(8,128)(2,1)} %copy-done.24) | copy-start | bytes 2359300
  472.3 202.1 %copy-start.47 = (f32[5,1024]{1,0:T(8,128)}, f32[5,1024]{1,0:T(8,128)S(1)}, u32[]{:S(2)}) copy-start(f32[5,1024]{1,0:T(8,128)S(1)} %stack.32) | copy-start | bytes 61444
  670.5 7.0 copy-start.16
  674.4 8.9 copy-start
  677.4 7.2 slice-start.2
  677.4 7.2 slice-start.3
  677.4 7.2 copy-start.77
  677.4 50.2 %copy-start.72 = (f32[1024]{0:T(1024)S(1)}, f32[1024]{0:T(1024)}, u32[]{:S(2)}) copy-start(f32[1024]{0:T(1024)} %get-tuple-element.802) | copy-start | bytes 12292
  (38 other events, 136.0 us)
Sparse Core Ops, SparseCore 0:
  9.6 104.7 all-gather.5
  116.0 48.6 all-gather.7
  387.7 59.9 reduce-scatter.12
  450.7 219.6 all-reduce.4
  673.9 163.6 reduce-scatter.6
  841.4 64.7 reduce-scatter.8
  910.4 94.4 reduce-scatter.10
